TPU v7x, 32 devices: a whole 2x2x4 slice. The times are simulated.
32 devices in a mesh: seq: 4 (over z), batch: 4 (over x, core), tensor: 2 (over y).
Axes of the slice: x: 2, y: 2, z: 4, core: 2. Of those that a mesh axis runs over, the one named last changes fastest.
Arguments:
- inputs: bfloat16 [4, 1024, 768], P('batch', 'seq'), may hold values from -16 to 16
- history: bfloat16 [8, 4, 1024, 768], P(None, 'batch', 'seq'), may hold values from -6 to 6
- window_lengths: int32 [4, 3], P('batch'), may hold values from 1 to 768, 1024 in all within a row
- block_order: int32 [4], replicated, may hold values from 0 to 3, each once
- first_gain: float32 [768], replicated, may hold values from 0.5 to 1.5
- first_shift: float32 [768], replicated, may hold values from -1.5 to 1.5
- query_weight: bfloat16 [768, 768], P(None, 'tensor'), may hold values from -0.21875 to 0.21875
- key_weight: bfloat16 [768, 768], P(None, 'tensor'), may hold values from -0.21875 to 0.21875
- value_weight: bfloat16 [768, 768], P(None, 'tensor'), may hold values from -0.21875 to 0.21875
- out_weight: bfloat16 [768, 768], P('tensor'), may hold values from -1.75 to 1.75
- second_gain: float32 [768], replicated, may hold values from 0.5 to 1.5
- second_shift: float32 [768], replicated, may hold values from -1.5 to 1.5
- up_weight: bfloat16 [768, 3072], P(None, 'tensor'), may hold values from -0.21875 to 0.21875
- up_bias: float32 [3072], P('tensor'), may hold values from -2.5 to 2.5
- down_weight: bfloat16 [3072, 768], P('tensor'), may hold values from -0.109375 to 0.109375
- down_bias: float32 [768], replicated, may hold values from -1.5 to 1.5
- mix_weights: float32 [9], replicated, may hold values from -2.5 to 2.5
- cotangent_next: bfloat16 [4, 1024, 768], P('batch', 'seq'), may hold values from -6 to 6
- cotangent_block: bfloat16 [4, 1024, 768], P('batch', 'seq'), may hold values from -6 to 6
Outputs:
- next_input: bfloat16 [4, 1024, 768], P('batch', 'seq')
- block_output: bfloat16 [4, 1024, 768], P('batch', 'seq')
- grad_input: bfloat16 [4, 1024, 768], P('batch', 'seq')
- grad_history: bfloat16 [8, 4, 1024, 768], P(None, 'batch', 'seq')
- grad_first_gain: float32 [768], replicated
- grad_first_shift: float32 [768], replicated
- grad_query_weight: float32 [768, 768], P(('seq', 'batch'), 'tensor')
- grad_key_weight: float32 [768, 768], P(('seq', 'batch'), 'tensor')
- grad_value_weight: float32 [768, 768], P(('seq', 'batch'), 'tensor')
- grad_out_weight: float32 [768, 768], P('tensor', ('seq', 'batch'))
- grad_second_gain: float32 [768], replicated
- grad_second_shift: float32 [768], replicated
- grad_up_weight: float32 [768, 3072], P(('seq', 'batch'), 'tensor')
- grad_up_bias: float32 [3072], P('tensor')
- grad_down_weight: float32 [3072, 768], P('tensor', ('seq', 'batch'))
- grad_down_bias: float32 [768], replicated
- grad_mix_weights: float32 [9], replicated
- rms_values: float32 [3], replicated
Inputs may be any that keep to these rules, and one draw needn't show every extreme that they name: `window_lengths`: each row sums to 1024; the longest window of each row has exactly 768 tokens. A permutation; index i of seq holds positions block_order[i] * 256 to block_order[i] * 256 + 255 of each sequence.
All inputs are finite; a program needn't handle non-finite values.
Results may differ from a plain program's by a relative error of at most 0.025.
Values may be sent and summed in bfloat16 or wider, within the bound.
A program may use at most 192 MiB of HBM per device.

v0:
```python
import jax
import jax.numpy as jnp
from jax import lax
from jax.sharding import PartitionSpec as P

HEAD_DIM = 64
epsilon = 1e-05


def layer_parts(values, gain, shift):
    centre = jnp.mean(values, axis=-1, keepdims=True)
    centred = values - centre
    spread = jnp.mean(centred * centred, axis=-1, keepdims=True)
    inverse = lax.rsqrt(spread + epsilon)
    unit = centred * inverse
    return (unit * gain + shift, unit, inverse)


def norm_backward(grad_out, unit, inverse, gain):
    scaled = grad_out * gain
    return inverse * (
        scaled
        - jnp.mean(scaled, axis=-1, keepdims=True)
        - unit * jnp.mean(scaled * unit, axis=-1, keepdims=True)
    )


def gelu_tanh(values):
    return (
        0.5
        * values
        * (1.0 + jnp.tanh(0.7978845608028654 * (values + 0.044715 * values * values * values)))
    )


def rotate(values, cosine, sine):
    half = values.shape[-1] // 2
    first = values[..., :half]
    second = values[..., half:]
    return jnp.concatenate(
        [first * cosine - second * sine, second * cosine + first * sine], axis=-1
    )


def keep_state(state):
    return state


def per_device(
    inputs,
    history,
    window_lengths,
    block_order,
    first_gain,
    first_shift,
    query_weight,
    key_weight,
    value_weight,
    out_weight,
    second_gain,
    second_shift,
    up_weight,
    up_bias,
    down_weight,
    down_bias,
    mix_weights,
    cotangent_next,
    cotangent_block,
):
    rows = inputs.shape[1]
    width = inputs.shape[2]
    local_width = query_weight.shape[1]
    heads = local_width // HEAD_DIM
    half = HEAD_DIM // 2
    depth = history.shape[0]
    total = rows * lax.axis_size("seq")
    size = min(1024, total)
    count = total // size
    split = (rows, heads, HEAD_DIM)
    offsets = jnp.arange(rows, dtype=jnp.int32)
    own_pos = block_order[lax.axis_index("seq")] * rows + offsets
    every_row = jnp.arange(total, dtype=jnp.int32)
    every_pos = block_order[every_row // rows] * rows + every_row % rows
    ends = jnp.cumsum(window_lengths[0])
    own_docs = jnp.sum((own_pos[:, None] >= ends[None, :]).astype(jnp.int32), axis=1)
    every_docs = jnp.sum((every_pos[:, None] >= ends[None, :]).astype(jnp.int32), axis=1)
    rates = jnp.exp(-jnp.log(10000.0) * jnp.arange(half, dtype=jnp.float32) / half)
    angles = own_pos.astype(jnp.float32)[:, None] * rates[None, :]
    cosine = jnp.cos(angles)[:, None, :]
    sine = jnp.sin(angles)[:, None, :]
    residual = inputs[0].astype(jnp.float32)
    normed_first, unit_first, scale_first = layer_parts(residual, first_gain, first_shift)
    normed_first = normed_first.astype(jnp.bfloat16)
    query_lin = jnp.dot(normed_first, query_weight, preferred_element_type=jnp.float32)
    key_lin = jnp.dot(normed_first, key_weight, preferred_element_type=jnp.float32)
    value_lin = jnp.dot(normed_first, value_weight, preferred_element_type=jnp.float32)
    queries = (rotate(query_lin.reshape(split), cosine, sine) * 0.125).astype(jnp.bfloat16)
    keys = (
        rotate(key_lin.reshape(split), cosine, sine).reshape(rows, local_width).astype(jnp.bfloat16)
    )
    values = value_lin.astype(jnp.bfloat16)
    all_keys, all_values = (
        lax.all_gather(keys, "seq", axis=0, tiled=True),
        lax.all_gather(values, "seq", axis=0, tiled=True),
    )

    def block_mask(index):
        key_pos = lax.dynamic_slice_in_dim(every_pos, index * size, size)
        key_docs = lax.dynamic_slice_in_dim(every_docs, index * size, size)
        return (key_pos[None, :] <= own_pos[:, None]) & (key_docs[None, :] == own_docs[:, None])

    def block_rows(array, index):
        return lax.dynamic_slice_in_dim(array, index * size, size).reshape(size, heads, HEAD_DIM)

    def block_scores(index, key_rows):
        return jnp.einsum(
            "qhd,khd->hqk", queries, block_rows(key_rows, index), preferred_element_type=jnp.float32
        )

    def stats_step(index, carry):
        allowed = block_mask(index)

        def update(state):
            peak, denom = state
            masked = jnp.where(allowed[None], block_scores(index, all_keys), -1e30)
            fresh = jnp.maximum(peak, jnp.max(masked, axis=-1))
            weights = jnp.where(allowed[None], jnp.exp(masked - fresh[..., None]), 0.0)
            return (fresh, denom * jnp.exp(peak - fresh) + jnp.sum(weights, axis=-1))

        return lax.cond(jnp.any(allowed), update, keep_state, carry)

    start_stats = (
        jnp.full((heads, rows), -1e30, jnp.float32),
        jnp.zeros((heads, rows), jnp.float32),
    )
    peak, denom = lax.fori_loop(0, count, stats_step, start_stats)

    def block_probs(index, allowed, key_rows):
        scores = block_scores(index, key_rows)
        return jnp.where(allowed[None], jnp.exp(scores - peak[..., None]), 0.0) / denom[..., None]

    def output_step(index, carry):
        allowed = block_mask(index)

        def output_accumulate(state):
            probs_low = block_probs(index, allowed, all_keys).astype(jnp.bfloat16)
            return state + jnp.einsum(
                "hqk,khd->qhd",
                probs_low,
                block_rows(all_values, index),
                preferred_element_type=jnp.float32,
            )

        return lax.cond(jnp.any(allowed), output_accumulate, keep_state, carry)

    running = lax.fori_loop(0, count, output_step, jnp.zeros(split, jnp.float32))
    mixed = running.reshape(rows, local_width).astype(jnp.bfloat16)
    attn_out = lax.psum(
        jnp.dot(mixed, out_weight, preferred_element_type=jnp.float32).astype(jnp.bfloat16),
        "tensor",
    ).astype(jnp.float32)
    hidden = residual + attn_out
    normed_second, unit_second, scale_second = layer_parts(hidden, second_gain, second_shift)
    normed_second = normed_second.astype(jnp.bfloat16)
    upward = jnp.dot(normed_second, up_weight, preferred_element_type=jnp.float32) + up_bias
    active_full, gelu_pull = jax.vjp(gelu_tanh, upward)
    active = active_full.astype(jnp.bfloat16)
    mlp_out = (
        lax.psum(
            jnp.dot(active, down_weight, preferred_element_type=jnp.float32).astype(jnp.bfloat16),
            "tensor",
        ).astype(jnp.float32)
        + down_bias
    )
    block_value = hidden + mlp_out
    history_low = history[:, 0]
    next_value = (
        jnp.sum(mix_weights[:depth, None, None] * history_low.astype(jnp.float32), axis=0)
        + mix_weights[depth] * block_value
    )
    cot_low = cotangent_next[0]
    cot_next = cot_low.astype(jnp.float32)
    cot_block = cotangent_block[0].astype(jnp.float32)
    grad_history = (mix_weights[:depth, None, None] * cot_next[None]).astype(jnp.bfloat16)
    mix_terms = jnp.concatenate(
        [
            jnp.einsum("jsd,sd->j", history_low, cot_low, preferred_element_type=jnp.float32),
            jnp.sum(block_value * cot_next)[None],
        ]
    )
    grad_block = cot_block + mix_weights[depth] * cot_next
    grad_mlp = grad_block.astype(jnp.bfloat16)
    grad_down = jnp.einsum("sf,sd->fd", active, grad_mlp, preferred_element_type=jnp.float32)
    grad_active = jnp.einsum("sd,fd->sf", grad_mlp, down_weight, preferred_element_type=jnp.float32)
    grad_up = gelu_pull(grad_active)[0].astype(jnp.bfloat16)
    grad_upw = jnp.einsum("sd,sf->df", normed_second, grad_up, preferred_element_type=jnp.float32)
    grad_normed_second = lax.psum(
        jnp.einsum("sf,df->sd", grad_up, up_weight, preferred_element_type=jnp.float32).astype(
            jnp.bfloat16
        ),
        "tensor",
    ).astype(jnp.float32)
    grad_hidden = grad_block + norm_backward(
        grad_normed_second, unit_second, scale_second, second_gain
    )
    grad_attn = grad_hidden.astype(jnp.bfloat16)
    grad_outw = jnp.einsum("sk,sd->kd", mixed, grad_attn, preferred_element_type=jnp.float32)
    grad_mixed = (
        jnp.einsum("sd,kd->sk", grad_attn, out_weight, preferred_element_type=jnp.float32)
        .astype(jnp.bfloat16)
        .reshape(split)
    )
    back_keys, back_values = (
        lax.all_gather(keys, "seq", axis=0, tiled=True),
        lax.all_gather(values, "seq", axis=0, tiled=True),
    )

    def delta_step(index, carry):
        allowed = block_mask(index)

        def delta_accumulate(state):
            probs = block_probs(index, allowed, back_keys)
            grad_probs = jnp.einsum(
                "qhd,khd->hqk",
                grad_mixed,
                block_rows(back_values, index),
                preferred_element_type=jnp.float32,
            )
            return state + jnp.sum(probs * grad_probs, axis=-1)

        return lax.cond(jnp.any(allowed), delta_accumulate, keep_state, carry)

    delta = lax.fori_loop(0, count, delta_step, jnp.zeros((heads, rows), jnp.float32))

    def grad_step(index, carry):
        allowed = block_mask(index)

        def grad_accumulate(state):
            grad_queries, key_buffer, value_buffer = state
            key_rows = block_rows(back_keys, index)
            value_rows = block_rows(back_values, index)
            probs = block_probs(index, allowed, back_keys)
            grad_probs = jnp.einsum(
                "qhd,khd->hqk", grad_mixed, value_rows, preferred_element_type=jnp.float32
            )
            grad_scores = (probs * (grad_probs - delta[..., None])).astype(jnp.bfloat16)
            grad_queries = grad_queries + jnp.einsum(
                "hqk,khd->qhd", grad_scores, key_rows, preferred_element_type=jnp.float32
            )
            key_part = jnp.einsum(
                "hqk,qhd->khd", grad_scores, queries, preferred_element_type=jnp.float32
            ).reshape(size, local_width)
            value_part = jnp.einsum(
                "hqk,qhd->khd",
                probs.astype(jnp.bfloat16),
                grad_mixed,
                preferred_element_type=jnp.float32,
            ).reshape(size, local_width)
            key_buffer = lax.dynamic_update_slice_in_dim(key_buffer, key_part, index * size, 0)
            value_buffer = lax.dynamic_update_slice_in_dim(
                value_buffer, value_part, index * size, 0
            )
            return (grad_queries, key_buffer, value_buffer)

        return lax.cond(jnp.any(allowed), grad_accumulate, keep_state, carry)

    start_grads = (
        jnp.zeros(split, jnp.float32),
        jnp.zeros((total, local_width), jnp.float32),
        jnp.zeros((total, local_width), jnp.float32),
    )
    grad_queries, key_buffer, value_buffer = lax.fori_loop(0, count, grad_step, start_grads)
    grad_keys, grad_values = (
        lax.psum_scatter(
            key_buffer.astype(jnp.bfloat16), "seq", scatter_dimension=0, tiled=True
        ).astype(jnp.float32),
        lax.psum_scatter(
            value_buffer.astype(jnp.bfloat16), "seq", scatter_dimension=0, tiled=True
        ).astype(jnp.float32),
    )
    grad_query_lin = (
        rotate(grad_queries * 0.125, cosine, -sine).reshape(rows, local_width).astype(jnp.bfloat16)
    )
    grad_key_lin = (
        rotate(grad_keys.reshape(split), cosine, -sine)
        .reshape(rows, local_width)
        .astype(jnp.bfloat16)
    )
    grad_value_lin = grad_values.astype(jnp.bfloat16)
    grad_queryw = jnp.einsum(
        "sd,se->de", normed_first, grad_query_lin, preferred_element_type=jnp.float32
    )
    grad_keyw = jnp.einsum(
        "sd,se->de", normed_first, grad_key_lin, preferred_element_type=jnp.float32
    )
    grad_valuew = jnp.einsum(
        "sd,se->de", normed_first, grad_value_lin, preferred_element_type=jnp.float32
    )
    local_normed = jnp.einsum(
        "se,de->sd", grad_query_lin, query_weight, preferred_element_type=jnp.float32
    )
    local_normed = local_normed + jnp.einsum(
        "se,de->sd", grad_key_lin, key_weight, preferred_element_type=jnp.float32
    )
    local_normed = local_normed + jnp.einsum(
        "se,de->sd", grad_value_lin, value_weight, preferred_element_type=jnp.float32
    )
    grad_normed_first = lax.psum(local_normed.astype(jnp.bfloat16), "tensor").astype(jnp.float32)
    grad_input = grad_hidden + norm_backward(grad_normed_first, unit_first, scale_first, first_gain)
    shared_grads = (
        lax.psum_scatter(grad_queryw, ("seq", "batch"), scatter_dimension=0, tiled=True),
        lax.psum_scatter(grad_keyw, ("seq", "batch"), scatter_dimension=0, tiled=True),
        lax.psum_scatter(grad_valuew, ("seq", "batch"), scatter_dimension=0, tiled=True),
        lax.psum_scatter(grad_outw, ("seq", "batch"), scatter_dimension=1, tiled=True),
        lax.psum_scatter(grad_upw, ("seq", "batch"), scatter_dimension=0, tiled=True),
        lax.psum_scatter(grad_down, ("seq", "batch"), scatter_dimension=1, tiled=True),
    )
    square_terms = jnp.stack(
        [
            jnp.sum(block_value * block_value),
            jnp.sum(attn_out * attn_out),
            jnp.sum(mlp_out * mlp_out),
        ]
    )
    small_terms = lax.psum(
        (
            jnp.sum(grad_normed_first * unit_first, axis=0),
            jnp.sum(grad_normed_first, axis=0),
            jnp.sum(grad_normed_second * unit_second, axis=0),
            jnp.sum(grad_normed_second, axis=0),
            jnp.sum(grad_up.astype(jnp.float32), axis=0),
            jnp.sum(grad_mlp.astype(jnp.float32), axis=0),
            mix_terms,
            square_terms,
        ),
        ("seq", "batch"),
    )
    entries = float(lax.axis_size("batch") * total * width)
    rms_values = jnp.sqrt(small_terms[7] / entries)
    return (
        next_value.astype(jnp.bfloat16)[None],
        block_value.astype(jnp.bfloat16)[None],
        grad_input.astype(jnp.bfloat16)[None],
        grad_history[:, None],
        small_terms[0],
        small_terms[1],
        shared_grads[0],
        shared_grads[1],
        shared_grads[2],
        shared_grads[3],
        small_terms[2],
        small_terms[3],
        shared_grads[4],
        small_terms[4],
        shared_grads[5],
        small_terms[5],
        small_terms[6],
        rms_values,
    )


def solution(mesh):
    in_specs = (
        P("batch", "seq", None),
        P(None, "batch", "seq", None),
        P("batch", None),
        P(),
        P(),
        P(),
        P(None, "tensor"),
        P(None, "tensor"),
        P(None, "tensor"),
        P("tensor", None),
        P(),
        P(),
        P(None, "tensor"),
        P("tensor"),
        P("tensor", None),
        P(),
        P(),
        P("batch", "seq", None),
        P("batch", "seq", None),
    )
    out_specs = (
        P("batch", "seq", None),
        P("batch", "seq", None),
        P("batch", "seq", None),
        P(None, "batch", "seq", None),
        P(),
        P(),
        P(("seq", "batch"), "tensor"),
        P(("seq", "batch"), "tensor"),
        P(("seq", "batch"), "tensor"),
        P("tensor", ("seq", "batch")),
        P(),
        P(),
        P(("seq", "batch"), "tensor"),
        P("tensor"),
        P("tensor", ("seq", "batch")),
        P(),
        P(),
        P(),
    )
    return jax.shard_map(
        per_device, mesh=mesh, in_specs=in_specs, out_specs=out_specs, check_vma=False
    )
```

profile of v0, /device:TPU:0, one launch (start us, length us, event | category | flops | bytes accessed | tf_op | source)
XLA Modules:
  0.0 684.2 jit_solution(1408262053932993367)
XLA Ops:
  9.9 2.1 copy.54
  13.2 2.3 fusion.53
  15.4 2.4 fusion.55
  19.9 2.1 multiply_subtract_fusion.2
  22.0 21.7 %all_gather.8 = bf16[1024,384]{0,1:T(8,128)(2,1)} all-gather(bf16[256,384]{0,1:T(8,128)(2,1)S(1)} %bitcast.211), channel_id=1, replica_groups=mesh['seq'=4,'batch'=4,'tensor'=2] {'seq'}, dimensions={0}, use_global_device_ids=true | all-gather | bytes 983040 | tf_op jit(solution)/shard_map/all_gather | solution.py:103
  43.7 2.6 fusion.67
  46.7 1.6 fusion.82
  49.5 17.3 %all_gather.9 = bf16[1024,384]{1,0:T(8,128)(2,1)S(1)} all-gather(bf16[256,384]{1,0:T(8,128)(2,1)S(1)} %convolution_convert_fusion.4), channel_id=1, replica_groups=mesh['seq'=4,'batch'=4,'tensor'=2] {'seq'}, dimensions={0}, use_global_device_ids=true | all-gather | bytes 983040 | tf_op jit(solution)/shard_map/all_gather | solution.py:104
  68.1 6.7 conditional.4
  68.1 2.1 select_reduce_fusion.1
  71.0 1.9 select_reduce_fusion
  75.6 6.0 conditional.5
  76.7 4.8 fusion.4
  83.3 2.2 convolution_convert_fusion.2
  87.0 3.2 convert_reduce_fusion.4
  90.3 21.2 %all-reduce.6.cloned.1.call-done = bf16[256,768]{1,0:T(8,128)(2,1)} async-done(((bf16[256,768]{1,0:T(8,128)(2,1)}), bf16[256,768]{1,0:T(8,128)(2,1)}) %all-reduce.6.cloned.1.call-update) | async-done | bytes 393232 | tf_op jit(solution)/shard_map/psum | solution.py:158
  114.5 2.7 convolution_add_fusion
  117.3 1.8 convolution_convert_fusion.1
  119.1 2.4 convert_reduce_fusion
  124.0 2.8 multiply_reduce_fusion.2
  126.8 31.8 %all-reduce.10.cloned.1.call-done = (bf16[256,768]{1,0:T(8,128)(2,1)}, bf16[256,768]{1,0:T(8,128)(2,1)}) async-done(((bf16[256,768]{1,0:T(8,128)(2,1)}, bf16[256,768]{1,0:T(8,128)(2,1)}), (bf16[256,768]{1,0:T(8,128)(2,1)}, bf16[256,768]{1,0:T(8,128)(2,1)})) %all-reduce.10.cloned.1.call-update) | async-done | bytes 786448 | tf_op jit(solution)/shard_map/psum | solution.py:169
  158.7 4.3 multiply_reduce_fusion.4
  165.3 1.8 copy.56
  167.0 11.1 %conditional.6 = (f32[6,256]{1,0:T(8,128)S(1)}) conditional(s32[]{:T(128)} %convert_element_type.198, f32[6,256]{1,0:T(8,128)S(1)} %broadcast.362, (pred[256,1024]{1,0:T(8,128)(4,1)}, bf16[1024,384]{0,1:T(8,128)(2,1)S(1)}, bf16[256,6,64]{0,2,1:T(8,128)(2,1)}, f32[6,256]{1,0:T(8,128)}, f32[6,256]{1,0:T(8,128)}, ...), branch_computations={%region_20.21_spmd, %region_21.23_spmd} | conditional | flops 410517504 | bytes 16420872 | solution.py:231
  167.0 4.6 fusion.84
  172.8 5.3 multiply_reduce_fusion
  178.1 17.4 %conditional.7 = (f32[256,6,64]{0,2,1:T(8,128)}, bf16[1024,384]{0,1:T(8,128)(2,1)}, bf16[1024,384]{0,1:T(8,128)(2,1)S(1)}) conditional(s32[]{:T(128)} %convert_element_type.198, f32[256,6,64]{0,2,1:T(8,128)} %broadcast.358, (pred[256,1024]{1,0:T(8,128)(4,1)}, bf16[1024,384]{0,1:T(8,128)(2,1)S(1)}, bf16[256,6,64]{0,2,1:T(8,128)(2,1)}, ...), branch_computations={%region_23.24_spmd, %region_24.25_spmd} | conditional | flops 1017741312 | bytes 61622352 | solution.py:265
  178.4 5.5 select_divide_fusion
  185.1 4.2 multiply_convert_fusion
  189.3 2.6 fusion.85
  191.9 2.9 fusion.8
  197.5 21.5 %reduce-scatter.9.cloned.1.call-done = bf16[256,384]{0,1:T(8,128)(2,1)} async-done(((bf16[1024,384]{0,1:T(8,128)(2,1)}), bf16[256,384]{0,1:T(8,128)(2,1)}) %reduce-scatter.9.cloned.1.call-update) | async-done | bytes 196624 | tf_op jit(solution)/shard_map/reduce_scatter | solution.py:274
  222.4 21.4 %reduce-scatter.11.cloned.1.call-done = bf16[256,384]{0,1:T(8,128)(2,1)} async-done(((bf16[1024,384]{0,1:T(8,128)(2,1)}), bf16[256,384]{0,1:T(8,128)(2,1)}) %reduce-scatter.11.cloned.1.call-update) | async-done | bytes 196624 | tf_op jit(solution)/shard_map/reduce_scatter | solution.py:277
  243.8 2.3 fusion.15
  251.1 1.6 fusion.72
  252.9 3.1 fusion.64
  257.4 3.1 fusion.75
  261.2 2.5 multiply_convert_fusion.1
  266.0 2.4 pad_maximum_fusion.2
  268.4 3.1 all-reduce.8.cloned.1.call-done
  271.5 2.0 fusion.46
  273.5 62.1 %all-reduce = (f32[768]{0:T(1024)}, f32[768]{0:T(1024)}, f32[768]{0:T(1024)}, f32[768]{0:T(1024)}, f32[1536]{0:T(1024)}, /*index=5*/f32[768]{0:T(1024)}, f32[9]{0:T(128)}, f32[3]{0:T(128)}) all-reduce(f32[768]{0:T(1024)} %get-tuple-element.439, ...), channel_id=1, replica_groups=mesh['seq'=4,'batch'=4,'tensor'=2] {'seq','batch'}, use_global_device_ids=true, to_apply=%region_31.32 | all-reduce | flops 5388 | bytes 43104 | tf_op jit(solution)/shard_map/psum | solution.py:325
  338.1 2.1 fusion.51
  340.1 55.5 %reduce-scatter.15.cloned.1.call-done = f32[48,384]{1,0:T(8,128)} async-done(((f32[768,384]{1,0:T(8,128)}), f32[48,384]{1,0:T(8,128)}) %reduce-scatter.15.cloned.1.call-update) | async-done | bytes 73744 | tf_op jit(solution)/shard_map/reduce_scatter | solution.py:312
  395.6 61.9 %reduce-scatter.13.cloned.1.call-done = f32[48,384]{1,0:T(8,128)} async-done(((f32[768,384]{1,0:T(8,128)}), f32[48,384]{1,0:T(8,128)}) %reduce-scatter.13.cloned.1.call-update) | async-done | bytes 73744 | tf_op jit(solution)/shard_map/reduce_scatter | solution.py:311
  457.5 61.7 %reduce-scatter.17.cloned.1.call-done = f32[48,384]{1,0:T(8,128)} async-done(((f32[768,384]{1,0:T(8,128)}), f32[48,384]{1,0:T(8,128)}) %reduce-scatter.17.cloned.1.call-update) | async-done | bytes 73744 | tf_op jit(solution)/shard_map/reduce_scatter | solution.py:313
  519.2 79.4 %reduce-scatter.21.cloned.1.call-done = f32[48,1536]{1,0:T(8,128)} async-done(((f32[768,1536]{1,0:T(8,128)}), f32[48,1536]{1,0:T(8,128)}) %reduce-scatter.21.cloned.1.call-update) | async-done | bytes 294928 | tf_op jit(solution)/shard_map/reduce_scatter | solution.py:315
  598.6 79.1 %reduce-scatter.23.cloned.1.call-done = f32[1536,48]{0,1:T(8,128)} async-done(((f32[1536,768]{0,1:T(8,128)}), f32[1536,48]{0,1:T(8,128)}) %reduce-scatter.23.cloned.1.call-update) | async-done | bytes 294928 | tf_op jit(solution)/shard_map/reduce_scatter | solution.py:316
  (203 shorter events, 42.9 us)
Async XLA Ops:
  7.2 110.0 %copy-start = (bf16[1536,768]{1,0:T(8,128)(2,1)S(1)}, bf16[1536,768]{1,0:T(8,128)(2,1)}, u32[]{:S(2)}) copy-start(bf16[1536,768]{1,0:T(8,128)(2,1)} %param.41) | copy-start | bytes 7077892
  7.2 5.9 copy-start.2
  7.2 4.8 copy-start.17
  7.2 5.9 copy-start.39
  7.2 5.9 copy-start.43
  7.3 104.2 %all-reduce.6.cloned.1.call-start = ((), (), s32[]{:S(2)}) async-start(), calls=%async_computation.8 | async-start | bytes 786432 | tf_op jit(solution)/shard_map/psum | solution.py:158
  8.7 40.3 %copy-start.41 = (f32[256]{0:T(256)}, f32[256]{0:T(256)S(1)}, u32[]{:S(2)}) copy-start(f32[256]{0:T(256)S(1)} %broadcast_multiply_fusion.6) | copy-start | bytes 3076
  9.9 39.0 %copy-start.45 = (f32[256]{0:T(256)}, f32[256]{0:T(256)S(1)}, u32[]{:S(2)}) copy-start(f32[256]{0:T(256)S(1)} %add_rsqrt_fusion.1) | copy-start | bytes 3076
  12.1 5.7 copy-start.57
  15.4 30.9 %copy-start.62 = (s32[1,3]{1,0:T(1,128)S(1)}, s32[1,3]{1,0:T(1,128)}, u32[]{:S(2)}) copy-start(s32[1,3]{1,0:T(1,128)} %param.29) | copy-start | bytes 40
  15.4 33.5 %copy-start.34 = (bf16[768,384]{1,0:T(8,128)(2,1)S(1)}, bf16[768,384]{1,0:T(8,128)(2,1)}, u32[]{:S(2)}) copy-start(bf16[768,384]{1,0:T(8,128)(2,1)} %param.35) | copy-start | bytes 1769476
  19.9 23.8 %copy-start.35 = (f32[256,32]{0,1:T(8,128)}, f32[256,32]{0,1:T(8,128)S(1)}, u32[]{:S(2)}) copy-start(f32[256,32]{0,1:T(8,128)S(1)} %get-tuple-element.485) | copy-start | bytes 98308
  49.0 17.8 %copy-start.31 = (f32[256,6,32]{0,2,1:T(8,128)S(1)}, f32[256,6,32]{0,2,1:T(8,128)}, u32[]{:S(2)}) copy-start(f32[256,6,32]{0,2,1:T(8,128)} %get-tuple-element.473) | copy-start | bytes 589828
  49.0 17.8 %copy-start.32 = (f32[256,6,32]{0,2,1:T(8,128)S(1)}, f32[256,6,32]{0,2,1:T(8,128)}, u32[]{:S(2)}) copy-start(f32[256,6,32]{0,2,1:T(8,128)} %get-tuple-element.474) | copy-start | bytes 589828
  49.0 19.1 %copy-start.8 = (bf16[1024,384]{0,1:T(8,128)(2,1)S(1)}, bf16[1024,384]{0,1:T(8,128)(2,1)}, u32[]{:S(2)}) copy-start(bf16[1024,384]{0,1:T(8,128)(2,1)} %all_gather.8) | copy-start | bytes 2359300
  49.0 19.1 %copy-start.16 = (pred[256,1024]{1,0:T(8,128)(4,1)S(1)}, pred[256,1024]{1,0:T(8,128)(4,1)}, u32[]{:S(2)}) copy-start(pred[256,1024]{1,0:T(8,128)(4,1)} %get-tuple-element.464) | copy-start | bytes 786436
  81.6 32.9 %copy-start.37 = (f32[768]{0:T(1024)S(1)}, f32[768]{0:T(1024)}, u32[]{:S(2)}) copy-start(f32[768]{0:T(1024)} %param.37) | copy-start | bytes 9220
  85.5 73.1 %all-reduce.10.cloned.1.call-start = ((), (), s32[]{:S(2)}) async-start(), calls=%async_computation.18 | async-start | bytes 1572864 | tf_op jit(solution)/shard_map/psum | solution.py:169
  123.9 34.7 %copy-start.4 = (bf16[256,768]{1,0:T(8,128)(2,1)S(1)}, bf16[256,768]{1,0:T(8,128)(2,1)}, u32[]{:S(2)}) copy-start(bf16[256,768]{1,0:T(8,128)(2,1)} %all-reduce.6.cloned.1.call-done) | copy-start | bytes 1179652
  123.9 34.7 %copy-start.10 = (bf16[1,256,768]{2,1,0:T(8,128)(2,1)S(1)}, bf16[1,256,768]{2,1,0:T(8,128)(2,1)}, u32[]{:S(2)}) copy-start(bf16[1,256,768]{2,1,0:T(8,128)(2,1)} %param.44) | copy-start | bytes 1179652
  123.9 34.7 %copy-start.49 = (f32[256]{0:T(256)S(1)}, f32[256]{0:T(256)}, u32[]{:S(2)}) copy-start(f32[256]{0:T(256)} %copy-done.48) | copy-start | bytes 3076
  123.9 34.7 %copy-start.53 = (f32[256]{0:T(256)S(1)}, f32[256]{0:T(256)}, u32[]{:S(2)}) copy-start(f32[256]{0:T(256)} %copy-done.52) | copy-start | bytes 3076
  123.9 34.8 %copy-start.58 = (f32[768]{0:T(1024)S(1)}, f32[768]{0:T(1024)}, u32[]{:S(2)}) copy-start(f32[768]{0:T(1024)} %param.42) | copy-start | bytes 9220
  124.0 95.0 %reduce-scatter.9.cloned.1.call-start = ((), (), s32[]{:S(2)}) async-start(), calls=%async_computation.9 | async-start | bytes 983040 | tf_op jit(solution)/shard_map/reduce_scatter | solution.py:274
  158.6 4.3 copy-start.25
  158.7 4.3 copy-start.26
  158.7 4.3 copy-start.50
  158.7 4.3 copy-start.54
  158.7 5.5 copy-start.14
  163.0 4.0 copy-start.9
  164.2 82.0 %copy-start.6 = (f32[256,768]{1,0:T(8,128)}, f32[256,768]{1,0:T(8,128)S(1)}, u32[]{:S(2)}) copy-start(f32[256,768]{1,0:T(8,128)S(1)} %fusion.39) | copy-start | bytes 2359300
  189.3 5.5 copy-start.3
  195.5 24.5 %copy-start.36 = (f32[256,32]{0,1:T(8,128)S(1)}, f32[256,32]{0,1:T(8,128)}, u32[]{:S(2)}) copy-start(f32[256,32]{0,1:T(8,128)} %copy-done.35) | copy-start | bytes 98308
  195.5 24.5 %copy-start.38 = (f32[256,32]{0,1:T(8,128)S(1)}, f32[256,32]{0,1:T(8,128)}, u32[]{:S(2)}) copy-start(f32[256,32]{0,1:T(8,128)} %get-tuple-element.483) | copy-start | bytes 98308
  195.5 24.7 %copy-start.15 = (bf16[768,384]{1,0:T(8,128)(2,1)S(1)}, bf16[768,384]{1,0:T(8,128)(2,1)}, u32[]{:S(2)}) copy-start(bf16[768,384]{1,0:T(8,128)(2,1)} %param.33) | copy-start | bytes 1769476
  195.6 48.2 %reduce-scatter.11.cloned.1.call-start = ((), (), s32[]{:S(2)}) async-start(), calls=%async_computation.10 | async-start | bytes 983040 | tf_op jit(solution)/shard_map/reduce_scatter | solution.py:277
  196.4 75.1 %all-reduce.8.cloned.1.call-start = ((), (), s32[]{:S(2)}) async-start(), calls=%async_computation.11 | async-start | bytes 786432 | tf_op jit(solution)/shard_map/psum | solution.py:308
  222.4 23.8 %copy-start.19 = (bf16[256,6,64]{0,2,1:T(8,128)(2,1)S(1)}, bf16[256,6,64]{0,2,1:T(8,128)(2,1)}, u32[]{:S(2)}) copy-start(bf16[256,6,64]{0,2,1:T(8,128)(2,1)} %copy-done.18) | copy-start | bytes 589828
  246.1 94.0 %reduce-scatter.19.cloned.1.call-start = ((), (), s32[]{:S(2)}) async-start(), calls=%async_computation.15 | async-start | bytes 1253376 | tf_op jit(solution)/shard_map/reduce_scatter | solution.py:314
  247.7 147.9 %reduce-scatter.15.cloned.1.call-start = ((), (), s32[]{:S(2)}) async-start(), calls=%async_computation.13 | async-start | bytes 1253376 | tf_op jit(solution)/shard_map/reduce_scatter | solution.py:312
  249.4 208.1 %reduce-scatter.13.cloned.1.call-start = ((), (), s32[]{:S(2)}) async-start(), calls=%async_computation.12 | async-start | bytes 1253376 | tf_op jit(solution)/shard_map/reduce_scatter | solution.py:311
  251.1 268.1 %reduce-scatter.17.cloned.1.call-start = ((), (), s32[]{:S(2)}) async-start(), calls=%async_computation.14 | async-start | bytes 1253376 | tf_op jit(solution)/shard_map/reduce_scatter | solution.py:313
  252.8 345.8 %reduce-scatter.21.cloned.1.call-start = ((), (), s32[]{:S(2)}) async-start(), calls=%async_computation.16 | async-start | bytes 5013504 | tf_op jit(solution)/shard_map/reduce_scatter | solution.py:315
  256.0 421.7 %reduce-scatter.23.cloned.1.call-start = ((), (), s32[]{:S(2)}) async-start(), calls=%async_computation.17 | async-start | bytes 5013504 | tf_op jit(solution)/shard_map/reduce_scatter | solution.py:316
  263.8 7.7 %copy-start.47 = (f32[256]{0:T(256)S(1)}, f32[256]{0:T(256)}, u32[]{:S(2)}) copy-start(f32[256]{0:T(256)} %copy-done.45) | copy-start | bytes 3076
  263.8 9.8 %copy-start.56 = (f32[768]{0:T(1024)S(1)}, f32[768]{0:T(1024)}, u32[]{:S(2)}) copy-start(f32[768]{0:T(1024)} %get-tuple-element.459) | copy-start | bytes 9220
  263.8 74.3 %copy-start.7 = (f32[256,768]{1,0:T(8,128)S(1)}, f32[256,768]{1,0:T(8,128)}, u32[]{:S(2)}) copy-start(f32[256,768]{1,0:T(8,128)} %copy-done.6) | copy-start | bytes 2359300
  263.8 413.9 %copy-start.1 = (bf16[1536,768]{1,0:T(8,128)(2,1)S(1)}, bf16[1536,768]{1,0:T(8,128)(2,1)}, u32[]{:S(2)}) copy-start(bf16[1536,768]{1,0:T(8,128)(2,1)} %param.41) | copy-start | bytes 7077892
  (26 other events, 41.3 us)
Sparse Core Ops, SparseCore 0:
  85.7 25.7 all-reduce.5
  124.1 34.5 all-reduce.9
  195.7 23.2 reduce-scatter.8
  221.2 22.5 reduce-scatter.10
  246.5 24.9 all-reduce.7
  276.0 58.0 reduce-scatter.18
  338.7 56.8 reduce-scatter.14
  400.3 57.1 reduce-scatter.12
  462.1 57.0 reduce-scatter.16
  524.0 74.5 reduce-scatter.20
  603.0 74.5 reduce-scatter.22
where the time goes:
time: 685 us; the launch traced here: 684 us
  waiting for transfers between devices  437 us (64%)
  blocking collectives  101 us (15%)
  matrix products  66.3 us (10%)
  other arithmetic  45.6 us (7%)
  local copies, waits for them, and re-layouts  17.4 us (3%)
  between operations  15.9 us (2%)
    reduce_scatter x1, waiting for transfers between devices, per_device(): lax.psum_scatter(grad_upw, ('seq', 'batch'), scatter_dimension=0, tiled=T...  79.4 us
    reduce_scatter x1, waiting for transfers between devices, per_device(): lax.psum_scatter(grad_down, ('seq', 'batch'), scatter_dimension=1, tiled=...  79.1 us
    psum x1, blocking collectives, per_device(): lax.psum((jnp.sum(grad_normed_first * unit_first, axis=0), jnp.sum(grad_n...  62.1 us
    reduce_scatter x1, waiting for transfers between devices, per_device(): lax.psum_scatter(grad_queryw, ('seq', 'batch'), scatter_dimension=0, tile...  61.9 us
    reduce_scatter x1, waiting for transfers between devices, per_device(): lax.psum_scatter(grad_valuew, ('seq', 'batch'), scatter_dimension=0, tile...  61.7 us
    reduce_scatter x1, waiting for transfers between devices, per_device(): lax.psum_scatter(grad_keyw, ('seq', 'batch'), scatter_dimension=0, tiled=...  55.5 us
    psum x1, waiting for transfers between devices, per_device(): lax.psum(jnp.dot(active, down_weight, preferred_element_type=jnp.float32)...  31.8 us
    all_gather x1, blocking collectives, per_device(): lax.all_gather(keys, 'seq', axis=0, tiled=True)  21.7 us
  transfers between devices with their start and end apart: 11, of which 10 were waited for; matrix products, arithmetic and copies ran while one was open for 5% of the time, Pallas kernels for 0%

commit v1 on v0

--- a/solution.py
+++ b/solution.py
@@ -155,9 +155,12 @@
 
     running = lax.fori_loop(0, count, output_step, jnp.zeros(split, jnp.float32))
     mixed = running.reshape(rows, local_width).astype(jnp.bfloat16)
-    attn_out = lax.psum(
-        jnp.dot(mixed, out_weight, preferred_element_type=jnp.float32).astype(jnp.bfloat16),
-        "tensor",
+    attn_out = jnp.sum(
+        lax.all_gather(
+            jnp.dot(mixed, out_weight, preferred_element_type=jnp.float32).astype(jnp.bfloat16),
+            "tensor",
+        ),
+        axis=0,
     ).astype(jnp.float32)
     hidden = residual + attn_out
     normed_second, unit_second, scale_second = layer_parts(hidden, second_gain, second_shift)

time: 685 us -> 665 us (0.971)
  waiting for transfers between devices: 437 us -> 414 us
  blocking collectives: 101 us -> 110 us
    psum x1 -> x0, waiting for transfers between devices: 21.2 us -> none  [per_device(): lax.psum(jnp.dot(mixed, out_weight, preferred_element_type=jnp.float32).a...]
    all_gather x0 -> x1, blocking collectives: none -> 8.74 us  [per_device(): lax.all_gather(jnp.dot(mixed, out_weight, preferred_element_type=jnp.floa...]
  transfers between devices with their start and end apart: 11 -> 10, of which waited for: 10 -> 9; matrix products, arithmetic and copies ran while one was open for 5% -> 5% of each run, Pallas kernels for 0% -> 0%
where the time goes in v1:
time: 665 us; the launch traced here: 663 us
  waiting for transfers between devices  414 us (62%)
  blocking collectives  110 us (17%)
  matrix products  64 us (10%)
  other arithmetic  43 us (6%)
  between operations  16.2 us (2%)
  local copies, waits for them, and re-layouts  15.8 us (2%)
    reduce_scatter x1, waiting for transfers between devices, per_device(): lax.psum_scatter(grad_down, ('seq', 'batch'), scatter_dimension=1, tiled=...  79.4 us
    reduce_scatter x1, waiting for transfers between devices, per_device(): lax.psum_scatter(grad_upw, ('seq', 'batch'), scatter_dimension=0, tiled=T...  79 us
    psum x1, blocking collectives, per_device(): lax.psum((jnp.sum(grad_normed_first * unit_first, axis=0), jnp.sum(grad_n...  61.8 us
    reduce_scatter x1, waiting for transfers between devices, per_device(): lax.psum_scatter(grad_valuew, ('seq', 'batch'), scatter_dimension=0, tile...  61.3 us
    reduce_scatter x1, waiting for transfers between devices, per_device(): lax.psum_scatter(grad_queryw, ('seq', 'batch'), scatter_dimension=0, tile...  61.3 us
    reduce_scatter x1, waiting for transfers between devices, per_device(): lax.psum_scatter(grad_keyw, ('seq', 'batch'), scatter_dimension=0, tiled=...  54.8 us
    psum x1, waiting for transfers between devices, per_device(): lax.psum(jnp.dot(active, down_weight, preferred_element_type=jnp.float32)...  32 us
    all_gather x1, blocking collectives, per_device(): lax.all_gather(keys, 'seq', axis=0, tiled=True)  21.7 us
  transfers between devices with their start and end apart: 10, of which 9 were waited for; matrix products, arithmetic and copies ran while one was open for 5% of the time, Pallas kernels for 0%

profile of v1, /device:TPU:0, one launch (start us, length us, event | category | flops | bytes accessed | tf_op | source)
XLA Modules:
  0.0 663.4 jit_solution(17510489261005983989)
XLA Ops:
  9.9 2.1 copy.54
  13.2 2.3 fusion.53
  15.5 2.3 fusion.55
  19.9 2.1 multiply_subtract_fusion.2
  22.0 21.7 %all_gather.14 = bf16[1024,384]{0,1:T(8,128)(2,1)} all-gather(bf16[256,384]{0,1:T(8,128)(2,1)S(1)} %bitcast.213), channel_id=1, replica_groups=mesh['seq'=4,'batch'=4,'tensor'=2] {'seq'}, dimensions={0}, use_global_device_ids=true | all-gather | bytes 983040 | tf_op jit(solution)/shard_map/all_gather | solution.py:103
  43.7 2.6 fusion.67
  46.7 1.6 fusion.82
  49.5 17.3 %all_gather.15 = bf16[1024,384]{1,0:T(8,128)(2,1)S(1)} all-gather(bf16[256,384]{1,0:T(8,128)(2,1)S(1)} %convolution_convert_fusion.4), channel_id=1, replica_groups=mesh['seq'=4,'batch'=4,'tensor'=2] {'seq'}, dimensions={0}, use_global_device_ids=true | all-gather | bytes 983040 | tf_op jit(solution)/shard_map/all_gather | solution.py:104
  68.2 6.7 %conditional.4 = (f32[6,256]{1,0:T(8,128)}, f32[6,256]{1,0:T(8,128)}) conditional(s32[]{:T(128)} %convert_element_type.200, (f32[6,256]{1,0:T(8,128)}, f32[6,256]{1,0:T(8,128)S(1)}) %tuple.66, (pred[256,1024]{1,0:T(8,128)(4,1)S(1)}, bf16[1024,384]{0,1:T(8,128)(2,1)S(1)}, bf16[256,6,64]{0,2,1:T(8,128)(2,1)}, f32[6,256]{1,0:T(8,128)}, ...), branch_computations={%region_7.8_spmd, %region_8.11_spmd} | conditional | flops 210766848 | bytes 14170128 | solution.py:130
  68.2 2.1 select_reduce_fusion.1
  71.0 1.9 select_reduce_fusion
  75.7 5.3 conditional.5
  76.8 4.1 fusion.4
  82.5 8.7 %all-gather = bf16[512,768]{1,0:T(8,128)(2,1)} all-gather(bf16[256,768]{1,0:T(8,128)(2,1)S(1)} %convolution_convert_fusion.2), channel_id=2, replica_groups=mesh['seq'=4,'batch'=4,'tensor'=2] {'tensor'}, dimensions={0}, use_global_device_ids=true | all-gather | bytes 1179648 | tf_op jit(solution)/shard_map/all_gather | solution.py:159
  93.7 2.5 convolution_add_fusion
  96.3 1.8 convolution_convert_fusion.1
  99.5 2.4 convert_reduce_fusion
  104.4 2.7 multiply_reduce_fusion.2
  107.1 32.0 %all-reduce.7.cloned.1.call-done = (bf16[256,768]{1,0:T(8,128)(2,1)}, bf16[256,768]{1,0:T(8,128)(2,1)}) async-done(((bf16[256,768]{1,0:T(8,128)(2,1)}, bf16[256,768]{1,0:T(8,128)(2,1)}), (bf16[256,768]{1,0:T(8,128)(2,1)}, bf16[256,768]{1,0:T(8,128)(2,1)})) %all-reduce.7.cloned.1.call-update) | async-done | bytes 786448 | tf_op jit(solution)/shard_map/psum | solution.py:172
  139.1 4.3 multiply_reduce_fusion.4
  145.7 1.7 copy.56
  147.5 11.1 %conditional.6 = (f32[6,256]{1,0:T(8,128)S(1)}) conditional(s32[]{:T(128)} %convert_element_type.200, f32[6,256]{1,0:T(8,128)S(1)} %broadcast.362, (pred[256,1024]{1,0:T(8,128)(4,1)}, bf16[1024,384]{0,1:T(8,128)(2,1)S(1)}, bf16[256,6,64]{0,2,1:T(8,128)(2,1)}, f32[6,256]{1,0:T(8,128)}, f32[6,256]{1,0:T(8,128)}, ...), branch_computations={%region_20.21_spmd, %region_21.23_spmd} | conditional | flops 410517504 | bytes 16420872 | solution.py:234
  147.5 4.6 fusion.84
  153.2 5.3 multiply_reduce_fusion
  158.6 16.6 %conditional.7 = (f32[256,6,64]{0,2,1:T(8,128)}, bf16[1024,384]{0,1:T(8,128)(2,1)S(1)}, bf16[1024,384]{0,1:T(8,128)(2,1)S(1)}) conditional(s32[]{:T(128)} %convert_element_type.200, f32[256,6,64]{0,2,1:T(8,128)} %broadcast.358, (pred[256,1024]{1,0:T(8,128)(4,1)}, bf16[1024,384]{0,1:T(8,128)(2,1)S(1)}, bf16[256,6,64]{0,2,1:T(8,128)(2,1)}, ...), branch_computations={%region_23.24_spmd, %region_24.25_spmd} | conditional | flops 1017741312 | bytes 61622352 | solution.py:268
  158.8 5.5 select_divide_fusion
  165.5 4.2 multiply_convert_fusion
  169.8 1.7 fusion.85
  171.5 3.0 fusion.8
  178.0 21.6 %reduce-scatter.9.cloned.1.call-done = bf16[256,384]{0,1:T(8,128)(2,1)} async-done(((bf16[1024,384]{0,1:T(8,128)(2,1)}), bf16[256,384]{0,1:T(8,128)(2,1)}) %reduce-scatter.9.cloned.1.call-update) | async-done | bytes 196624 | tf_op jit(solution)/shard_map/reduce_scatter | solution.py:277
  203.7 20.9 %reduce-scatter.11.cloned.1.call-done = bf16[256,384]{0,1:T(8,128)(2,1)} async-done(((bf16[1024,384]{0,1:T(8,128)(2,1)}), bf16[256,384]{0,1:T(8,128)(2,1)}) %reduce-scatter.11.cloned.1.call-update) | async-done | bytes 196624 | tf_op jit(solution)/shard_map/reduce_scatter | solution.py:280
  224.6 2.3 fusion.15
  228.6 1.6 fusion.57
  230.3 1.6 fusion.59
  232.0 1.6 fusion.72
  233.7 3.1 fusion.64
  238.3 3.1 fusion.75
  242.1 2.5 multiply_convert_fusion.1
  246.9 2.5 pad_maximum_fusion.2
  249.4 3.1 all-reduce.5.cloned.1.call-done
  252.5 2.0 fusion.46
  254.5 61.8 %all-reduce = (f32[768]{0:T(1024)}, f32[768]{0:T(1024)}, f32[768]{0:T(1024)}, f32[768]{0:T(1024)}, f32[1536]{0:T(1024)}, /*index=5*/f32[768]{0:T(1024)}, f32[9]{0:T(128)}, f32[3]{0:T(128)}) all-reduce(f32[768]{0:T(1024)} %get-tuple-element.439, ...), channel_id=1, replica_groups=mesh['seq'=4,'batch'=4,'tensor'=2] {'seq','batch'}, use_global_device_ids=true, to_apply=%region_31.32 | all-reduce | flops 5388 | bytes 43104 | tf_op jit(solution)/shard_map/psum | solution.py:328
  318.7 2.1 fusion.51
  320.8 54.8 %reduce-scatter.15.cloned.1.call-done = f32[48,384]{1,0:T(8,128)} async-done(((f32[768,384]{1,0:T(8,128)}), f32[48,384]{1,0:T(8,128)}) %reduce-scatter.15.cloned.1.call-update) | async-done | bytes 73744 | tf_op jit(solution)/shard_map/reduce_scatter | solution.py:315
  375.7 61.3 %reduce-scatter.13.cloned.1.call-done = f32[48,384]{1,0:T(8,128)} async-done(((f32[768,384]{1,0:T(8,128)}), f32[48,384]{1,0:T(8,128)}) %reduce-scatter.13.cloned.1.call-update) | async-done | bytes 73744 | tf_op jit(solution)/shard_map/reduce_scatter | solution.py:314
  436.9 61.3 %reduce-scatter.17.cloned.1.call-done = f32[48,384]{1,0:T(8,128)} async-done(((f32[768,384]{1,0:T(8,128)}), f32[48,384]{1,0:T(8,128)}) %reduce-scatter.17.cloned.1.call-update) | async-done | bytes 73744 | tf_op jit(solution)/shard_map/reduce_scatter | solution.py:316
  498.2 79.0 %reduce-scatter.21.cloned.1.call-done = f32[48,1536]{1,0:T(8,128)} async-done(((f32[768,1536]{1,0:T(8,128)}), f32[48,1536]{1,0:T(8,128)}) %reduce-scatter.21.cloned.1.call-update) | async-done | bytes 294928 | tf_op jit(solution)/shard_map/reduce_scatter | solution.py:318
  577.2 79.4 %reduce-scatter.23.cloned.1.call-done = f32[1536,48]{0,1:T(8,128)} async-done(((f32[1536,768]{0,1:T(8,128)}), f32[1536,48]{0,1:T(8,128)}) %reduce-scatter.23.cloned.1.call-update) | async-done | bytes 294928 | tf_op jit(solution)/shard_map/reduce_scatter | solution.py:319
  (210 shorter events, 40.6 us)
Async XLA Ops:
  7.2 89.0 %copy-start = (bf16[1536,768]{1,0:T(8,128)(2,1)S(1)}, bf16[1536,768]{1,0:T(8,128)(2,1)}, u32[]{:S(2)}) copy-start(bf16[1536,768]{1,0:T(8,128)(2,1)} %param.41) | copy-start | bytes 7077892
  7.2 6.0 copy-start.2
  7.2 4.8 copy-start.19
  7.2 5.9 copy-start.40
  7.2 5.9 copy-start.45
  7.3 131.8 %all-reduce.7.cloned.1.call-start = ((), (), s32[]{:S(2)}) async-start(), calls=%async_computation.17 | async-start | bytes 1572864 | tf_op jit(solution)/shard_map/psum | solution.py:172
  8.7 40.3 %copy-start.43 = (f32[256]{0:T(256)}, f32[256]{0:T(256)S(1)}, u32[]{:S(2)}) copy-start(f32[256]{0:T(256)S(1)} %broadcast_multiply_fusion.6) | copy-start | bytes 3076
  9.9 39.0 %copy-start.47 = (f32[256]{0:T(256)}, f32[256]{0:T(256)S(1)}, u32[]{:S(2)}) copy-start(f32[256]{0:T(256)S(1)} %add_rsqrt_fusion.1) | copy-start | bytes 3076
  12.1 5.7 copy-start.59
  15.5 30.9 %copy-start.66 = (s32[1,3]{1,0:T(1,128)S(1)}, s32[1,3]{1,0:T(1,128)}, u32[]{:S(2)}) copy-start(s32[1,3]{1,0:T(1,128)} %param.29) | copy-start | bytes 40
  15.5 33.5 %copy-start.37 = (bf16[768,384]{1,0:T(8,128)(2,1)S(1)}, bf16[768,384]{1,0:T(8,128)(2,1)}, u32[]{:S(2)}) copy-start(bf16[768,384]{1,0:T(8,128)(2,1)} %param.35) | copy-start | bytes 1769476
  19.9 23.8 %copy-start.38 = (f32[256,32]{0,1:T(8,128)}, f32[256,32]{0,1:T(8,128)S(1)}, u32[]{:S(2)}) copy-start(f32[256,32]{0,1:T(8,128)S(1)} %get-tuple-element.485) | copy-start | bytes 98308
  49.0 17.8 %copy-start.34 = (f32[256,6,32]{0,2,1:T(8,128)S(1)}, f32[256,6,32]{0,2,1:T(8,128)}, u32[]{:S(2)}) copy-start(f32[256,6,32]{0,2,1:T(8,128)} %get-tuple-element.473) | copy-start | bytes 589828
  49.0 17.8 %copy-start.35 = (f32[256,6,32]{0,2,1:T(8,128)S(1)}, f32[256,6,32]{0,2,1:T(8,128)}, u32[]{:S(2)}) copy-start(f32[256,6,32]{0,2,1:T(8,128)} %get-tuple-element.474) | copy-start | bytes 589828
  49.0 19.2 %copy-start.9 = (bf16[1024,384]{0,1:T(8,128)(2,1)S(1)}, bf16[1024,384]{0,1:T(8,128)(2,1)}, u32[]{:S(2)}) copy-start(bf16[1024,384]{0,1:T(8,128)(2,1)} %all_gather.14) | copy-start | bytes 2359300
  49.0 19.1 %copy-start.18 = (pred[256,1024]{1,0:T(8,128)(4,1)S(1)}, pred[256,1024]{1,0:T(8,128)(4,1)}, u32[]{:S(2)}) copy-start(pred[256,1024]{1,0:T(8,128)(4,1)} %get-tuple-element.464) | copy-start | bytes 786436
  66.8 8.8 %copy-start.4 = (bf16[1024,384]{1,0:T(8,128)(2,1)}, bf16[1024,384]{1,0:T(8,128)(2,1)S(1)}, u32[]{:S(2)}) copy-start(bf16[1024,384]{1,0:T(8,128)(2,1)S(1)} %all_gather.15) | copy-start | bytes 2359300
  80.9 10.3 %copy-start.20 = (bf16[256,6,64]{0,2,1:T(8,128)(2,1)}, bf16[256,6,64]{0,2,1:T(8,128)(2,1)S(1)}, u32[]{:S(2)}) copy-start(bf16[256,6,64]{0,2,1:T(8,128)(2,1)S(1)} %convert_element_type.208) | copy-start | bytes 589828
  80.9 12.1 %copy-start.61 = (f32[9]{0:T(128)S(1)}, f32[9]{0:T(128)}, u32[]{:S(2)}) copy-start(f32[9]{0:T(128)} %param.43) | copy-start | bytes 112
  81.0 12.7 %copy-start.39 = (f32[768]{0:T(1024)S(1)}, f32[768]{0:T(1024)}, u32[]{:S(2)}) copy-start(f32[768]{0:T(1024)} %param.37) | copy-start | bytes 9220
  81.0 12.7 %copy-start.41 = (f32[768]{0:T(1024)S(1)}, f32[768]{0:T(1024)}, u32[]{:S(2)}) copy-start(f32[768]{0:T(1024)} %param.38) | copy-start | bytes 9220
  81.0 12.7 %copy-start.65 = (f32[1536]{0:T(1024)S(1)}, f32[1536]{0:T(1024)}, u32[]{:S(2)}) copy-start(f32[1536]{0:T(1024)} %param.40) | copy-start | bytes 18436
  104.3 34.7 %copy-start.51 = (f32[256]{0:T(256)S(1)}, f32[256]{0:T(256)}, u32[]{:S(2)}) copy-start(f32[256]{0:T(256)} %copy-done.50) | copy-start | bytes 3076
  104.3 34.7 %copy-start.55 = (f32[256]{0:T(256)S(1)}, f32[256]{0:T(256)}, u32[]{:S(2)}) copy-start(f32[256]{0:T(256)} %copy-done.54) | copy-start | bytes 3076
  104.3 34.7 %copy-start.60 = (f32[768]{0:T(1024)S(1)}, f32[768]{0:T(1024)}, u32[]{:S(2)}) copy-start(f32[768]{0:T(1024)} %param.42) | copy-start | bytes 9220
  104.4 95.2 %reduce-scatter.9.cloned.1.call-start = ((), (), s32[]{:S(2)}) async-start(), calls=%async_computation.8 | async-start | bytes 983040 | tf_op jit(solution)/shard_map/reduce_scatter | solution.py:277
  139.1 4.3 copy-start.28
  139.1 4.3 copy-start.29
  139.1 4.3 copy-start.52
  139.1 4.3 copy-start.56
  139.1 5.5 copy-start.16
  143.4 4.1 copy-start.5
  144.6 82.4 %copy-start.7 = (f32[256,768]{1,0:T(8,128)}, f32[256,768]{1,0:T(8,128)S(1)}, u32[]{:S(2)}) copy-start(f32[256,768]{1,0:T(8,128)S(1)} %fusion.39) | copy-start | bytes 2359300
  169.8 4.7 copy-start.3
  176.1 48.5 %reduce-scatter.11.cloned.1.call-start = ((), (), s32[]{:S(2)}) async-start(), calls=%async_computation.9 | async-start | bytes 983040 | tf_op jit(solution)/shard_map/reduce_scatter | solution.py:280
  176.9 24.7 %copy-start.17 = (bf16[768,384]{1,0:T(8,128)(2,1)S(1)}, bf16[768,384]{1,0:T(8,128)(2,1)}, u32[]{:S(2)}) copy-start(bf16[768,384]{1,0:T(8,128)(2,1)} %param.33) | copy-start | bytes 1769476
  176.9 75.6 %all-reduce.5.cloned.1.call-start = ((), (), s32[]{:S(2)}) async-start(), calls=%async_computation.10 | async-start | bytes 786432 | tf_op jit(solution)/shard_map/psum | solution.py:311
  203.7 23.3 %copy-start.21 = (bf16[256,6,64]{0,2,1:T(8,128)(2,1)S(1)}, bf16[256,6,64]{0,2,1:T(8,128)(2,1)}, u32[]{:S(2)}) copy-start(bf16[256,6,64]{0,2,1:T(8,128)(2,1)} %copy-done.20) | copy-start | bytes 589828
  227.0 93.8 %reduce-scatter.19.cloned.1.call-start = ((), (), s32[]{:S(2)}) async-start(), calls=%async_computation.14 | async-start | bytes 1253376 | tf_op jit(solution)/shard_map/reduce_scatter | solution.py:317
  228.5 147.1 %reduce-scatter.15.cloned.1.call-start = ((), (), s32[]{:S(2)}) async-start(), calls=%async_computation.12 | async-start | bytes 1253376 | tf_op jit(solution)/shard_map/reduce_scatter | solution.py:315
  230.3 206.7 %reduce-scatter.13.cloned.1.call-start = ((), (), s32[]{:S(2)}) async-start(), calls=%async_computation.11 | async-start | bytes 1253376 | tf_op jit(solution)/shard_map/reduce_scatter | solution.py:314
  231.9 266.3 %reduce-scatter.17.cloned.1.call-start = ((), (), s32[]{:S(2)}) async-start(), calls=%async_computation.13 | async-start | bytes 1253376 | tf_op jit(solution)/shard_map/reduce_scatter | solution.py:316
  233.6 343.6 %reduce-scatter.21.cloned.1.call-start = ((), (), s32[]{:S(2)}) async-start(), calls=%async_computation.15 | async-start | bytes 5013504 | tf_op jit(solution)/shard_map/reduce_scatter | solution.py:318
  236.8 419.8 %reduce-scatter.23.cloned.1.call-start = ((), (), s32[]{:S(2)}) async-start(), calls=%async_computation.16 | async-start | bytes 5013504 | tf_op jit(solution)/shard_map/reduce_scatter | solution.py:319
  244.6 7.9 %copy-start.49 = (f32[256]{0:T(256)S(1)}, f32[256]{0:T(256)}, u32[]{:S(2)}) copy-start(f32[256]{0:T(256)} %copy-done.47) | copy-start | bytes 3076
  244.6 9.9 %copy-start.58 = (f32[768]{0:T(1024)S(1)}, f32[768]{0:T(1024)}, u32[]{:S(2)}) copy-start(f32[768]{0:T(1024)} %get-tuple-element.459) | copy-start | bytes 9220
  244.6 74.1 %copy-start.8 = (f32[256,768]{1,0:T(8,128)S(1)}, f32[256,768]{1,0:T(8,128)}, u32[]{:S(2)}) copy-start(f32[256,768]{1,0:T(8,128)} %copy-done.7) | copy-start | bytes 2359300
  244.6 412.0 %copy-start.1 = (bf16[1536,768]{1,0:T(8,128)(2,1)S(1)}, bf16[1536,768]{1,0:T(8,128)(2,1)}, u32[]{:S(2)}) copy-start(bf16[1536,768]{1,0:T(8,128)(2,1)} %param.41) | copy-start | bytes 7077892
  (29 other events, 51.3 us)
Sparse Core Ops, SparseCore 0:
  104.5 34.5 all-reduce.6
  176.2 23.3 reduce-scatter.8
  202.0 22.5 reduce-scatter.10
  227.4 24.9 all-reduce.4
  256.5 57.8 reduce-scatter.18
  318.5 57.1 reduce-scatter.14
  379.8 57.0 reduce-scatter.12
  441.1 57.0 reduce-scatter.16
  502.6 74.5 reduce-scatter.20
  582.0 74.5 reduce-scatter.22
